TPU v7x, 256 devices: a whole 4x4x8 slice. The times are simulated.
256 devices in a mesh: walk: 16 (over z, x_hi), blk: 16 (over x_lo, y, core).
Axes of the slice: x: 4 (x_hi: 2, x_lo: 2; x = x_hi * 2 + x_lo), y: 4, z: 8, core: 2. Of those that a mesh axis runs over, the one named last changes fastest.
Arguments:
- vertex_times: int32 [16, 1024], P('blk'), may hold values from 0 to 4095
- vertex_sites: int32 [16, 1024], P('blk'), may hold values from 0 to 15
- vertex_matrix: bfloat16 [16, 1024, 1024], P('blk', 'walk'), may hold values from -0.1875 to 0.1875
- bare_green: float32 [2, 1024], replicated, may hold values from -3 to 3
- transfer_momentum: int32 [16], replicated, may hold values from 0 to 15, each once
- transfers: int32 [32], replicated, may hold values from 0 to 31, each once
Outputs:
- g4: float32 [2, 32, 1024, 1024], P(None, 'blk', 'walk')
Inputs may be any that keep to these rules, and one draw needn't show every extreme that they name: `transfer_momentum`: each of 0 to 15 appears exactly once. `transfers`: each of 0 to 31 appears exactly once.
All inputs are finite; a program needn't handle non-finite values.
Results may differ from a plain program's by a relative error of at most 0.0071.
Values may be sent and summed in bfloat16 or wider, within the bound.
A program may use at most 64 MiB of HBM per device.

v0:
```python
import math
import jax
import jax.numpy as jnp
from jax import lax
from jax.sharding import PartitionSpec as P

NM = 16
NF = 64
NV = 1024
NT = 4096
QB = 2
side_length = 4


def fourier_table(times, sites):
    points = jnp.arange(NM * NF, dtype=jnp.int32)
    momentum = points // NF
    frequency = points % NF
    momentum_x = momentum // side_length
    momentum_y = momentum % side_length
    site_x = sites // side_length
    site_y = sites % side_length
    odd_part = 4 * (2 * frequency + 1 - NF)
    phase = odd_part[:, None] * times[None, :] - 2 * NT * (
        momentum_x[:, None] * site_x[None, :] + momentum_y[:, None] * site_y[None, :]
    )
    phase = jnp.mod(phase, 8 * NT)
    angle = phase.astype(jnp.float32) * (2.0 * math.pi / (8 * NT))
    return (jnp.cos(angle).astype(jnp.bfloat16), jnp.sin(angle).astype(jnp.bfloat16))


def assemble(spread_re, spread_im, row_re, row_im, col_re, col_im, rows, cols):
    scale = NV ** (-0.5)
    part_re = (spread_re * col_re[None, :] - spread_im * col_im[None, :]) * scale
    part_im = (spread_re * col_im[None, :] + spread_im * col_re[None, :]) * scale
    diagonal = (rows[:, None] == cols[None, :]).astype(jnp.float32)
    green_re = row_re[:, None] * (part_re + diagonal) - row_im[:, None] * part_im
    green_im = row_re[:, None] * part_im + row_im[:, None] * (part_re + diagonal)
    return (green_re.astype(jnp.bfloat16), green_im.astype(jnp.bfloat16))


def send_layout(panels, shift):
    count = panels.shape[0]
    row_count = panels.shape[2]
    grid = panels.reshape(count, 2, row_count, NM, NF)
    grid = jnp.take(grid, shift, axis=3)
    grid = jnp.transpose(grid, (0, 1, 3, 2, 4))
    return grid.reshape(count, 2, 1, NM, row_count * NF)


def receive_layout(incoming, shift):
    count, _, groups, moments, flat = incoming.shape
    row_count = flat // NF
    grid = incoming.reshape(count, 2, groups, moments, row_count, NF)
    grid = jnp.transpose(grid, (0, 1, 3, 5, 2, 4))
    grid = jnp.take(grid, shift, axis=4)
    return grid.reshape(count, 2, moments * NF, NM * NF)


def accumulate(total, direct, turned, offsets):
    moments = turned.shape[1] // NF
    grid = turned.reshape(2, moments, NF, NM, NF)
    near = direct.astype(jnp.float32)
    spots = jnp.arange(NF, dtype=jnp.int32)
    for position in range(offsets.shape[0]):
        offset = offsets[position]
        rolled = jnp.roll(grid, -offset, axis=2)
        rolled = jnp.roll(rolled, -offset, axis=4)
        valid = (spots + offset >= 0) & (spots + offset < NF)
        keep = valid[:, None, None] & valid[None, None, :]
        masked = jnp.where(keep[None, None], rolled, jnp.zeros((), rolled.dtype))
        shifted = masked.reshape(2, moments * NF, NM * NF).astype(jnp.float32)
        part_re = near[0] * shifted[0] - near[1] * shifted[1]
        part_im = near[0] * shifted[1] + near[1] * shifted[0]
        total = total.at[:, position].add(jnp.stack([part_re, part_im]))
    return total


def walker_sum(total, direct_panels, turned_panels, offsets):

    def step(carry, pair):
        return (accumulate(carry, pair[0], pair[1], offsets), None)

    result, _ = lax.scan(step, total, (direct_panels, turned_panels))
    return result


def shards(vertex_times, vertex_sites, vertex_matrix, bare_green, transfer_momentum, transfers):
    walk_count = lax.axis_size("walk")
    walk_index = lax.axis_index("walk")
    blk_index = lax.axis_index("blk")
    points = NM * NF
    row_count = points // walk_count
    four_re, four_im = fourier_table(vertex_times[0], vertex_sites[0])
    row_start = walk_index * row_count
    rows_re = lax.dynamic_slice_in_dim(four_re, row_start, row_count, 0)
    rows_im = lax.dynamic_slice_in_dim(four_im, row_start, row_count, 0)
    piece = lax.all_gather(vertex_matrix[0], "walk", axis=0, tiled=True)
    inner_re = jnp.dot(rows_re, piece, preferred_element_type=jnp.float32)
    inner_im = jnp.dot(rows_im, piece, preferred_element_type=jnp.float32)
    inner_re = inner_re.astype(jnp.bfloat16)
    inner_im = inner_im.astype(jnp.bfloat16)
    contract = (((1,), (1,)), ((), ()))

    def product(left, right):
        return lax.dot_general(left, right, contract, preferred_element_type=jnp.float32)

    spread_re = product(inner_re, four_re) + product(inner_im, four_im)
    spread_im = product(inner_im, four_re) - product(inner_re, four_im)
    rows = row_start + jnp.arange(row_count, dtype=jnp.int32)
    cols = jnp.arange(points, dtype=jnp.int32)
    row_re = lax.dynamic_slice_in_dim(bare_green[0], row_start, row_count)
    row_im = lax.dynamic_slice_in_dim(bare_green[1], row_start, row_count)
    green_re, green_im = assemble(
        spread_re, spread_im, row_re, row_im, bare_green[0], bare_green[1], rows, cols
    )
    direct = jnp.stack([green_re, green_im])
    window_size = transfers.shape[0]
    offsets = lax.dynamic_slice_in_dim(transfers, blk_index * QB, QB) - window_size // 2
    slab = jnp.zeros((2, QB, row_count, points), jnp.float32)
    outgoing = send_layout(direct[None], transfer_momentum)
    incoming = lax.all_to_all(outgoing, "walk", split_axis=3, concat_axis=2, tiled=True)
    turned = receive_layout(incoming, transfer_momentum)
    return walker_sum(
        slab,
        lax.all_gather(direct[None], "blk", axis=0, tiled=True),
        lax.all_gather(turned, "blk", axis=0, tiled=True),
        offsets,
    )


def solution(mesh):
    return jax.shard_map(
        shards,
        mesh=mesh,
        in_specs=(P("blk", None), P("blk", None), P("blk", "walk", None), P(), P(), P()),
        out_specs=P(None, "blk", "walk", None),
        check_vma=False,
    )
```

profile of v0, /device:TPU:1, one launch (start us, length us, event | category | flops | bytes accessed | tf_op | source)
XLA Modules:
  0.0 327.5 jit_solution(9244534965251903392)
XLA Ops:
  7.3 0.8 fusion.45
  8.9 20.5 %cosine_convert_fusion = (bf16[1024,1024]{1,0:T(8,128)(2,1)S(1)}, bf16[1024,1024]{1,0:T(8,128)(2,1)}) fusion(s32[1024]{0:T(1024)S(1)} %bitcast.120, s32[1024]{0:T(1024)S(1)} %get-tuple-element.158, s32[1024]{0:T(1024)S(1)} %bitcast.117, s32[1024]{0:T(1024)S(1)} %get-tuple-element.159, s32[1024]{0:T(1024)} %bitcast.125, s32[1024]{0:T(1024)S(1)} %fusion.25), kind=kLoop, calls=%fused_computation.38 | loop fusion | flops 22020096 | bytes 4218880 | tf_op jit(solution)/shard_map/convert_element_type | solution.py:29
  29.4 66.0 %all-gather.8.cloned.1.call-done = bf16[1,1024,1024]{2,1,0:T(8,128)(2,1)} async-done(((bf16[1,64,1024]{2,1,0:T(8,128)(2,1)}), bf16[1,1024,1024]{2,1,0:T(8,128)(2,1)}) %all-gather.8.cloned.1.call-update) | async-done | bytes 2097168 | tf_op jit(solution)/shard_map/all_gather | solution.py:98
  95.4 2.2 fusion.14
  97.7 0.8 fusion.47
  98.5 1.4 fusion.17
  99.9 0.8 fusion.48
  100.6 16.4 %convolution_add_fusion = f32[64,1024]{1,0:T(8,128)S(1)} fusion(f32[64,1024]{1,0:T(8,128)S(1)} %fusion.47, bf16[64,1024]{1,0:T(8,128)(2,1)S(1)} %fusion.17, s32[1024]{0:T(1024)S(1)} %bitcast.121, s32[1024]{0:T(1024)S(1)} %get-tuple-element.158, s32[1024]{0:T(1024)S(1)} %bitcast.118, s32[1024]{0:T(1024)S(1)} %get-tuple-element.159, s32[1024]{0:T(1024)S(1)} %bitcast.126, ...), kind=kOutput, calls=%fused_computation.44 | convolution fusion | flops 155254784 | bytes 679936 | tf_op jit(solution)/shard_map/dot_general | solution.py:106
  117.1 16.6 %subtract_convert_fusion = (bf16[64,1024]{1,0:T(8,128)(2,1)S(1)}, bf16[64,1024]{1,0:T(8,128)(2,1)S(1)}) fusion(f32[64]{0:T(128)S(1)} %get-tuple-element.156, f32[64]{0:T(128)S(1)} %get-tuple-element.129, f32[1024]{0:T(1024)S(1)} %bitcast.123, f32[64,1024]{1,0:T(8,128)S(1)} %convolution_add_fusion, f32[1024]{0:T(1024)S(1)} %bitcast.124, ...), kind=kOutput, calls=%fused_computation.52 | convolution fusion | flops 156434432 | bytes 951552 | tf_op jit(solution)/shard_map/dot_general | solution.py:106
  136.1 1.1 reshape.348
  137.3 4.0 %all-to-all-start = ((bf16[1,2,1,16,4096]{4,1,2,0,3:T(2,128)(2,1)}), bf16[1,2,1,16,4096]{4,1,2,0,3:T(2,128)(2,1)S(1)}, u32[]{:S(2)}, u32[]{:S(2)}) async-start(bf16[1,2,1,16,4096]{4,1,2,0,3:T(2,128)(2,1)} %bitcast.28), calls=%async_computation | async-start | bytes 524288 | tf_op jit(solution)/shard_map/all_to_all | solution.py:122
  141.5 11.0 %all-to-all-done = bf16[1,2,1,16,4096]{4,1,2,0,3:T(2,128)(2,1)S(1)} async-done(((bf16[1,2,1,16,4096]{4,1,2,0,3:T(2,128)(2,1)}), bf16[1,2,1,16,4096]{4,1,2,0,3:T(2,128)(2,1)S(1)}, u32[]{:S(2)}, u32[]{:S(2)}) %all-to-all-start) | async-done | bytes 262176 | tf_op jit(solution)/shard_map/all_to_all | solution.py:122
  157.3 18.6 %all-gather.10.cloned.1.call-done = bf16[32,64,1024]{2,1,0:T(8,128)(2,1)} async-done(((bf16[2,64,1024]{2,1,0:T(8,128)(2,1)}), bf16[32,64,1024]{2,1,0:T(8,128)(2,1)}) %all-gather.10.cloned.1.call-update) | async-done | bytes 4194320 | tf_op jit(solution)/shard_map/all_gather | solution.py:126
  175.9 41.9 %all-gather.6.cloned.1.call-done = bf16[16,2,64,1024]{3,2,1,0:T(8,128)(2,1)} async-done(((bf16[1,2,64,1024]{3,2,1,0:T(8,128)(2,1)}), bf16[16,2,64,1024]{3,2,1,0:T(8,128)(2,1)}) %all-gather.6.cloned.1.call-update) | async-done | bytes 4194320 | tf_op jit(solution)/shard_map/all_gather | solution.py:127
  218.0 101.8 %while.14 = (s32[]{:T(128)}, f32[2,2,64,1024]{3,2,1,0:T(8,128)S(1)}, bf16[16,2,64,1024]{3,2,1,0:T(8,128)(2,1)}, s32[2]{0:T(128)S(1)}, bf16[16,2,64,1024]{3,2,1,0...) while((s32[]{:T(128)}, ...), condition=%wide.region_1.4_spmd, body=%wide.region_0.3_spmd.sunk | while | flops 3023392 | bytes 18367192 | solution.py:84
  218.0 1.1 dynamic-slice_convert_fusion.2
  220.4 1.2 compare_and_fusion.4
  224.4 1.1 dynamic-slice_convert_fusion.2
  226.7 1.2 compare_and_fusion.4
  230.7 1.1 dynamic-slice_convert_fusion.2
  233.1 1.2 compare_and_fusion.4
  237.1 1.1 dynamic-slice_convert_fusion.2
  239.5 1.2 compare_and_fusion.4
  243.5 1.1 dynamic-slice_convert_fusion.2
  245.8 1.2 compare_and_fusion.4
  249.8 1.1 dynamic-slice_convert_fusion.2
  252.2 1.2 compare_and_fusion.4
  256.2 1.1 dynamic-slice_convert_fusion.2
  258.5 1.2 compare_and_fusion.4
  262.6 1.1 dynamic-slice_convert_fusion.2
  264.9 1.2 compare_and_fusion.4
  268.9 1.1 dynamic-slice_convert_fusion.2
  271.3 1.2 compare_and_fusion.4
  275.3 1.1 dynamic-slice_convert_fusion.2
  277.6 1.2 compare_and_fusion.4
  281.6 1.1 dynamic-slice_convert_fusion.2
  284.0 1.2 compare_and_fusion.4
  288.0 1.1 dynamic-slice_convert_fusion.2
  290.4 1.2 compare_and_fusion.4
  294.4 1.1 dynamic-slice_convert_fusion.2
  296.7 1.2 compare_and_fusion.4
  300.7 1.1 dynamic-slice_convert_fusion.2
  303.1 1.2 compare_and_fusion.4
  307.1 1.1 dynamic-slice_convert_fusion.2
  309.5 1.2 compare_and_fusion.4
  313.5 1.1 dynamic-slice_convert_fusion.2
  315.8 1.2 compare_and_fusion.4
  319.8 1.0 copy-done
  (347 shorter events, 70.2 us)
Async XLA Ops:
  6.5 88.9 %all-gather.8.cloned.1.call-start = ((), (), s32[]{:S(2)}) async-start(), calls=%async_computation.2 | async-start | bytes 2228224 | tf_op jit(solution)/shard_map/all_gather | solution.py:98
  7.3 168.7 %all-gather.10.cloned.1.call-start = ((), (), s32[]{:S(2)}) async-start(), calls=%async_computation.3 | async-start | bytes 4456448 | tf_op jit(solution)/shard_map/all_gather | solution.py:126
  95.4 3.0 copy-start.1
  97.7 2.9 copy-start.2
  117.0 17.4 %copy-start.3 = (s32[16]{0:T(128)S(1)}, s32[16]{0:T(128)}, u32[]{:S(2)}) copy-start(s32[16]{0:T(128)} %param.20) | copy-start | bytes 196
  136.0 19.3 %copy-start.4 = (s32[32]{0:T(128)S(1)}, s32[32]{0:T(128)}, u32[]{:S(2)}) copy-start(s32[32]{0:T(128)} %param.21) | copy-start | bytes 388
  137.3 15.2 %all-to-all-start = ((bf16[1,2,1,16,4096]{4,1,2,0,3:T(2,128)(2,1)}), bf16[1,2,1,16,4096]{4,1,2,0,3:T(2,128)(2,1)S(1)}, u32[]{:S(2)}, u32[]{:S(2)}) async-start(bf16[1,2,1,16,4096]{4,1,2,0,3:T(2,128)(2,1)} %bitcast.28), calls=%async_computation | async-start | bytes 524288 | tf_op jit(solution)/shard_map/all_to_all | solution.py:122
  141.3 76.5 %all-gather.6.cloned.1.call-start = ((), (), s32[]{:S(2)}) async-start(), calls=%async_computation.1 | async-start | bytes 4456448 | tf_op jit(solution)/shard_map/all_gather | solution.py:127
  319.8 1.0 copy-start
Sparse Core Ops, SparseCore 0:
  9.9 85.4 all-gather.7
  134.5 41.3 all-gather.9
  177.8 40.0 all-gather.5
where the time goes:
time: 331 us; the launch traced here: 328 us
  waiting for transfers between devices  138 us (42%)
  other arithmetic  88.1 us (27%)
  local copies, waits for them, and re-layouts  41.2 us (12%)
  matrix products  38.1 us (12%)
  between operations  14.9 us (5%)
  starting transfers between devices  4.11 us (1%)
    all_gather x1, waiting for transfers between devices, shards(): piece = lax.all_gather(vertex_matrix[0], 'walk', axis=0, tiled=True)  66 us
    all_gather x1, waiting for transfers between devices, shards(): lax.all_gather(turned, 'blk', axis=0, tiled=True)  41.9 us
    dot_general x4, matrix products, product(): lax.dot_general(left, right, contract, preferred_element_type=jnp.float32)  34.5 us
    convert_element_type x1, other arithmetic, fourier_table(): jnp.cos(angle).astype(jnp.bfloat16)  20.5 us
    convert_element_type x32, other arithmetic, accumulate(): shifted = masked.reshape(2, moments * NF, NM * NF).astype(jnp.float32)  19.8 us
    and x16, other arithmetic, accumulate(): valid = (spots + offset >= 0) & (spots + offset < NF)  19.1 us
    all_gather x1, waiting for transfers between devices, shards(): lax.all_gather(direct[None], 'blk', axis=0, tiled=True)  18.6 us
    convert_element_type x16, other arithmetic, accumulate(): near = direct.astype(jnp.float32)  17.6 us
  transfers between devices with their start and end apart: 4, of which 4 were waited for; matrix products, arithmetic and copies ran while one was open for 9% of the time, Pallas kernels for 0%

commit v1 on v0

--- a/solution.py
+++ b/solution.py
@@ -95,7 +95,10 @@
     row_start = walk_index * row_count
     rows_re = lax.dynamic_slice_in_dim(four_re, row_start, row_count, 0)
     rows_im = lax.dynamic_slice_in_dim(four_im, row_start, row_count, 0)
-    piece = lax.all_gather(vertex_matrix[0], "walk", axis=0, tiled=True)
+    piece = jnp.concatenate(
+        lax.all_to_all(jnp.stack([vertex_matrix[0]] * lax.psum(1, "walk"), axis=0), "walk", 0, 0),
+        axis=0,
+    )
     inner_re = jnp.dot(rows_re, piece, preferred_element_type=jnp.float32)
     inner_im = jnp.dot(rows_im, piece, preferred_element_type=jnp.float32)
     inner_re = inner_re.astype(jnp.bfloat16)

time: 331 us -> 306 us (0.924)
  waiting for transfers between devices: 138 us -> 98.4 us
  starting transfers between devices: 4.11 us -> 17.4 us
    all_gather x1 -> x0, waiting for transfers between devices: 66 us -> none  [shards(): piece = lax.all_gather(vertex_matrix[0], 'walk', axis=0, tiled=True)]
    all_to_all x0 -> x1, waiting for transfers between devices: none -> 30 us  [shards(): lax.all_to_all(jnp.stack([vertex_matrix[0]] * lax.psum(1, 'walk'), axis=0...]
    all_to_all x0 -> x1, starting transfers between devices: none -> 11.6 us  [shards(): lax.all_to_all(jnp.stack([vertex_matrix[0]] * lax.psum(1, 'walk'), axis=0...]
    all_gather x1, waiting for transfers between devices: 18.6 us -> 14.3 us  [shards(): lax.all_gather(direct[None], 'blk', axis=0, tiled=True)]
where the time goes in v1:
time: 306 us; the launch traced here: 302 us
  waiting for transfers between devices  98.4 us (32%)
  other arithmetic  86.7 us (28%)
  local copies, waits for them, and re-layouts  43 us (14%)
  matrix products  38.7 us (13%)
  starting transfers between devices  17.4 us (6%)
  between operations  15.2 us (5%)
    all_gather x1, waiting for transfers between devices, shards(): lax.all_gather(turned, 'blk', axis=0, tiled=True)  42.1 us
    dot_general x4, matrix products, product(): lax.dot_general(left, right, contract, preferred_element_type=jnp.float32)  34.5 us
    all_to_all x1, waiting for transfers between devices, shards(): lax.all_to_all(jnp.stack([vertex_matrix[0]] * lax.psum(1, 'walk'), axis=0...  30 us
    convert_element_type x32, other arithmetic, accumulate(): shifted = masked.reshape(2, moments * NF, NM * NF).astype(jnp.float32)  19.8 us
    convert_element_type x1, other arithmetic, fourier_table(): jnp.cos(angle).astype(jnp.bfloat16)  19.8 us
    and x16, other arithmetic, accumulate(): valid = (spots + offset >= 0) & (spots + offset < NF)  19.1 us
    convert_element_type x16, other arithmetic, accumulate(): near = direct.astype(jnp.float32)  17.6 us
    all_gather x1, waiting for transfers between devices, shards(): lax.all_gather(direct[None], 'blk', axis=0, tiled=True)  14.3 us
  transfers between devices with their start and end apart: 4, of which 4 were waited for; matrix products, arithmetic and copies ran while one was open for 9% of the time, Pallas kernels for 0%

profile of v1, /device:TPU:1, one launch (start us, length us, event | category | flops | bytes accessed | tf_op | source)
XLA Modules:
  0.0 302.2 jit_solution(17308348800461946594)
XLA Ops:
  6.5 2.5 stack.34
  9.0 11.6 %all-to-all-start = ((bf16[16,64,1024]{2,1,0:T(8,128)(2,1)}), bf16[16,64,1024]{2,1,0:T(8,128)(2,1)}, u32[]{:S(2)}, u32[]{:S(2)}) async-start(bf16[16,64,1024]{2,1,0:T(8,128)(2,1)} %stack.34), calls=%async_computation | async-start | bytes 4194304 | tf_op jit(solution)/shard_map/all_to_all | solution.py:99
  20.9 19.8 %cosine_convert_fusion = (bf16[1024,1024]{1,0:T(8,128)(2,1)S(1)}, bf16[1024,1024]{1,0:T(8,128)(2,1)}) fusion(s32[1024]{0:T(1024)S(1)} %bitcast.116, s32[1024]{0:T(1024)S(1)} %get-tuple-element.158, s32[1024]{0:T(1024)S(1)} %bitcast.113, s32[1024]{0:T(1024)S(1)} %get-tuple-element.159, s32[1024]{0:T(1024)S(1)} %bitcast.121, s32[1024]{0:T(1024)S(1)} %fusion.15), kind=kLoop, calls=%fused_computation.38 | loop fusion | flops 22020096 | bytes 4218880 | tf_op jit(solution)/shard_map/convert_element_type | solution.py:29
  40.7 30.0 %all-to-all-done = bf16[16,64,1024]{2,1,0:T(8,128)(2,1)} async-done(((bf16[16,64,1024]{2,1,0:T(8,128)(2,1)}), bf16[16,64,1024]{2,1,0:T(8,128)(2,1)}, u32[]{:S(2)}, u32[]{:S(2)}) %all-to-all-start) | async-done | bytes 2097184 | tf_op jit(solution)/shard_map/all_to_all | solution.py:99
  70.7 2.1 convolution_convert_fusion.1
  72.7 0.8 fusion.37
  73.5 2.2 convolution_convert_fusion
  76.4 16.4 %convolution_add_fusion = f32[64,1024]{1,0:T(8,128)S(1)} fusion(f32[64,1024]{1,0:T(8,128)S(1)} %fusion.37, bf16[64,1024]{1,0:T(8,128)(2,1)S(1)} %convolution_convert_fusion, s32[1024]{0:T(1024)S(1)} %bitcast.117, s32[1024]{0:T(1024)S(1)} %get-tuple-element.158, s32[1024]{0:T(1024)S(1)} %bitcast.114, s32[1024]{0:T(1024)S(1)} %get-tuple-element.159, ...), kind=kOutput, calls=%fused_computation.40 | convolution fusion | flops 155254784 | bytes 679936 | tf_op jit(solution)/shard_map/dot_general | solution.py:109
  92.9 16.6 %subtract_convert_fusion = (bf16[64,1024]{1,0:T(8,128)(2,1)S(1)}, bf16[64,1024]{1,0:T(8,128)(2,1)S(1)}) fusion(f32[64]{0:T(128)S(1)} %get-tuple-element.156, f32[64]{0:T(128)S(1)} %get-tuple-element.129, f32[1024]{0:T(1024)S(1)} %bitcast.119, f32[64,1024]{1,0:T(8,128)S(1)} %convolution_add_fusion, f32[1024]{0:T(1024)S(1)} %bitcast.120, ...), kind=kOutput, calls=%fused_computation.48 | convolution fusion | flops 156434432 | bytes 951552 | tf_op jit(solution)/shard_map/dot_general | solution.py:109
  111.9 1.1 reshape.352
  113.1 5.7 %all-to-all-start.1 = ((bf16[1,2,1,16,4096]{4,1,2,0,3:T(2,128)(2,1)}), bf16[1,2,1,16,4096]{4,1,2,0,3:T(2,128)(2,1)S(1)}, u32[]{:S(2)}, u32[]{:S(2)}) async-start(bf16[1,2,1,16,4096]{4,1,2,0,3:T(2,128)(2,1)} %bitcast.29), calls=%async_computation.1 | async-start | bytes 524288 | tf_op jit(solution)/shard_map/all_to_all | solution.py:125
  119.0 12.0 %all-to-all-done.1 = bf16[1,2,1,16,4096]{4,1,2,0,3:T(2,128)(2,1)S(1)} async-done(((bf16[1,2,1,16,4096]{4,1,2,0,3:T(2,128)(2,1)}), bf16[1,2,1,16,4096]{4,1,2,0,3:T(2,128)(2,1)S(1)}, u32[]{:S(2)}, u32[]{:S(2)}) %all-to-all-start.1) | async-done | bytes 262176 | tf_op jit(solution)/shard_map/all_to_all | solution.py:125
  135.8 14.3 %all-gather.6.cloned.1.call-done = bf16[32,64,1024]{2,1,0:T(8,128)(2,1)} async-done(((bf16[2,64,1024]{2,1,0:T(8,128)(2,1)}), bf16[32,64,1024]{2,1,0:T(8,128)(2,1)}) %all-gather.6.cloned.1.call-update) | async-done | bytes 4194320 | tf_op jit(solution)/shard_map/all_gather | solution.py:129
  150.0 42.1 %all-gather.4.cloned.1.call-done = bf16[16,2,64,1024]{3,2,1,0:T(8,128)(2,1)} async-done(((bf16[1,2,64,1024]{3,2,1,0:T(8,128)(2,1)}), bf16[16,2,64,1024]{3,2,1,0:T(8,128)(2,1)}) %all-gather.4.cloned.1.call-update) | async-done | bytes 4194320 | tf_op jit(solution)/shard_map/all_gather | solution.py:130
  192.3 101.8 %while.14 = (s32[]{:T(128)}, f32[2,2,64,1024]{3,2,1,0:T(8,128)S(1)}, bf16[16,2,64,1024]{3,2,1,0:T(8,128)(2,1)}, s32[2]{0:T(128)S(1)}, bf16[16,2,64,1024]{3,2,1,0...) while((s32[]{:T(128)}, ...), condition=%wide.region_1.4_spmd, body=%wide.region_0.3_spmd.sunk | while | flops 3023392 | bytes 18367192 | solution.py:84
  192.4 1.1 dynamic-slice_convert_fusion.2
  194.7 1.2 compare_and_fusion.4
  198.7 1.1 dynamic-slice_convert_fusion.2
  201.1 1.2 compare_and_fusion.4
  205.1 1.1 dynamic-slice_convert_fusion.2
  207.4 1.2 compare_and_fusion.4
  211.4 1.1 dynamic-slice_convert_fusion.2
  213.8 1.2 compare_and_fusion.4
  217.8 1.1 dynamic-slice_convert_fusion.2
  220.2 1.2 compare_and_fusion.4
  224.2 1.1 dynamic-slice_convert_fusion.2
  226.5 1.2 compare_and_fusion.4
  230.5 1.1 dynamic-slice_convert_fusion.2
  232.9 1.2 compare_and_fusion.4
  236.9 1.1 dynamic-slice_convert_fusion.2
  239.3 1.2 compare_and_fusion.4
  243.3 1.1 dynamic-slice_convert_fusion.2
  245.6 1.2 compare_and_fusion.4
  249.6 1.1 dynamic-slice_convert_fusion.2
  252.0 1.2 compare_and_fusion.4
  256.0 1.1 dynamic-slice_convert_fusion.2
  258.3 1.2 compare_and_fusion.4
  262.3 1.1 dynamic-slice_convert_fusion.2
  264.7 1.2 compare_and_fusion.4
  268.7 1.1 dynamic-slice_convert_fusion.2
  271.1 1.2 compare_and_fusion.4
  275.1 1.1 dynamic-slice_convert_fusion.2
  277.4 1.2 compare_and_fusion.4
  281.4 1.1 dynamic-slice_convert_fusion.2
  283.8 1.2 compare_and_fusion.4
  287.8 1.1 dynamic-slice_convert_fusion.2
  290.2 1.2 compare_and_fusion.4
  294.1 1.0 copy-done
  (349 shorter events, 69.5 us)
Async XLA Ops:
  6.5 14.2 %copy-start.1 = (f32[2,1024]{1,0:T(2,128)S(1)}, f32[2,1024]{1,0:T(2,128)}, u32[]{:S(2)}) copy-start(f32[2,1024]{1,0:T(2,128)} %param.19) | copy-start | bytes 24580
  6.5 14.3 %copy-start.2 = (s32[1,1024]{1,0:T(1,128)S(1)}, s32[1,1024]{1,0:T(1,128)}, u32[]{:S(2)}) copy-start(s32[1,1024]{1,0:T(1,128)} %param.17) | copy-start | bytes 12292
  6.5 14.4 %copy-start.3 = (s32[1,1024]{1,0:T(1,128)S(1)}, s32[1,1024]{1,0:T(1,128)}, u32[]{:S(2)}) copy-start(s32[1,1024]{1,0:T(1,128)} %param.16) | copy-start | bytes 12292
  9.0 61.6 %all-to-all-start = ((bf16[16,64,1024]{2,1,0:T(8,128)(2,1)}), bf16[16,64,1024]{2,1,0:T(8,128)(2,1)}, u32[]{:S(2)}, u32[]{:S(2)}) async-start(bf16[16,64,1024]{2,1,0:T(8,128)(2,1)} %stack.34), calls=%async_computation | async-start | bytes 4194304 | tf_op jit(solution)/shard_map/all_to_all | solution.py:99
  20.7 129.4 %all-gather.6.cloned.1.call-start = ((), (), s32[]{:S(2)}) async-start(), calls=%async_computation.3 | async-start | bytes 4456448 | tf_op jit(solution)/shard_map/all_gather | solution.py:129
  92.8 17.4 %copy-start.4 = (s32[16]{0:T(128)S(1)}, s32[16]{0:T(128)}, u32[]{:S(2)}) copy-start(s32[16]{0:T(128)} %param.20) | copy-start | bytes 196
  111.8 21.9 %copy-start.5 = (s32[32]{0:T(128)S(1)}, s32[32]{0:T(128)}, u32[]{:S(2)}) copy-start(s32[32]{0:T(128)} %param.21) | copy-start | bytes 388
  113.1 17.9 %all-to-all-start.1 = ((bf16[1,2,1,16,4096]{4,1,2,0,3:T(2,128)(2,1)}), bf16[1,2,1,16,4096]{4,1,2,0,3:T(2,128)(2,1)S(1)}, u32[]{:S(2)}, u32[]{:S(2)}) async-start(bf16[1,2,1,16,4096]{4,1,2,0,3:T(2,128)(2,1)} %bitcast.29), calls=%async_computation.1 | async-start | bytes 524288 | tf_op jit(solution)/shard_map/all_to_all | solution.py:125
  118.8 73.4 %all-gather.4.cloned.1.call-start = ((), (), s32[]{:S(2)}) async-start(), calls=%async_computation.2 | async-start | bytes 4456448 | tf_op jit(solution)/shard_map/all_gather | solution.py:130
  294.1 1.0 copy-start
Sparse Core Ops, SparseCore 0:
  110.3 39.6 all-gather.5
  151.9 40.2 all-gather.3
